TPU v7x, 256 devices: a whole 4x4x8 slice. The times are simulated.
256 devices in a mesh: ia: 8 (over z), ja: 32 (over y, x, core).
Axes of the slice: x: 4, y: 4, z: 8, core: 2. Of those that a mesh axis runs over, the one named last changes fastest.
Arguments:
- pno_basis: bfloat16 [8, 64, 512, 128], P('ia', 'ja'), may hold values from -0.4375 to 0.4375
- domain_map: int32 [8, 64, 512], replicated, may hold values from 0 to 1023, as said below
- amplitudes: float32 [8, 64, 128, 128], P('ia', 'ja'), may hold values from -6 to 6
- exchange_ints: float32 [8, 64, 128, 128], P('ia', 'ja'), may hold values from -6 to 6
- pno_energy: float32 [8, 64, 128], P('ia', 'ja'), may hold values from 0.5 to 3
- row_energy: float32 [8], P('ia'), may hold values from -1.5 to -0.3
- column_energy: float32 [64], P('ja'), may hold values from -1.5 to -0.3
- coupling_rows: float32 [8, 8], P('ia'), may hold values from -0.6 to 0.6
- coupling_columns: float32 [64, 64], P(None, 'ja'), may hold values from -0.6 to 0.6
- row_neighbours: int32 [8, 64, 6], P('ia', 'ja'), may hold values from 0 to 7, as said below
- column_neighbours: int32 [8, 64, 24], P('ia', 'ja'), may hold values from 0 to 63, as said below
- row_counts: int32 [8, 64], P('ia', 'ja'), may hold values from 1 to 6
- column_counts: int32 [8, 64], P('ia', 'ja'), may hold values from 1 to 24
Outputs:
- new_amplitudes: float32 [8, 64, 128, 128], P('ia', 'ja')
- pair_energy: float32 [8, 64], P('ia', 'ja')
Inputs may be any that keep to these rules, and one draw needn't show every extreme that they name: `domain_map`: the 512 entries of one pair are distinct. `row_neighbours`: the 6 entries of a pair (i, j) are distinct and differ from i. `column_neighbours`: the 24 entries of a pair (i, j) are distinct and differ from j.
All inputs are finite; a program needn't handle non-finite values.
Results may differ from a plain program's by a relative error of at most 0.008.
Values may be sent and summed in bfloat16 or wider, within the bound.
No kernel may reach another device: no remote copies, remote signals or barrier semaphores. Data moves between devices by JAX's collectives and lax.ppermute only.
A program may use at most 64 MiB of HBM per device.

v0:
```python
import jax
import jax.numpy as jnp
from jax import lax
from jax.sharding import PartitionSpec as P

ITERS = 2
level_shift = 0.3


def sent_to_all(shard, axis):
    copies = jnp.broadcast_to(shard, (lax.axis_size(axis), *shard.shape))
    return lax.all_to_all(copies, axis, split_axis=0, concat_axis=0, tiled=True)


def in_order(parts, dim):
    parts = jnp.moveaxis(parts, 0, dim)
    dims = parts.shape
    return parts.reshape(*dims[:dim], dims[dim] * dims[dim + 1], *dims[dim + 2 :])


def gathered_copies(shard, axis, dim):
    parts = sent_to_all(shard, axis)
    return in_order(parts, dim)


def pair_intersections(packed):
    own_domain, own_basis, partner_domains, partner_bases = packed
    match = (own_domain[None, :, None] == partner_domains[:, None, :]).astype(jnp.bfloat16)
    picked = jnp.einsum(
        "suv,svb->sub", match, partner_bases, preferred_element_type=jnp.float32
    ).astype(jnp.bfloat16)
    return jnp.einsum("ua,sub->sab", own_basis, picked, preferred_element_type=jnp.float32).astype(
        jnp.bfloat16
    )


def local(
    pno_basis,
    domain_map,
    amplitudes,
    exchange_ints,
    pno_energy,
    row_energy,
    column_energy,
    coupling_rows,
    coupling_columns,
    row_neighbours,
    column_neighbours,
    row_counts,
    column_counts,
):
    pair_rows = pno_basis.shape[0]
    pair_columns = pno_basis.shape[1]
    domain_size = pno_basis.shape[2]
    width = amplitudes.shape[-1]
    total_rows = domain_map.shape[0]
    total_columns = domain_map.shape[1]
    own_pairs = pair_rows * pair_columns
    row_offset = lax.axis_index("ia") * pair_rows
    column_offset = lax.axis_index("ja") * pair_columns
    domain_rows = lax.dynamic_slice_in_dim(domain_map, row_offset, pair_rows, 0)
    domain_columns = lax.dynamic_slice_in_dim(domain_map, column_offset, pair_columns, 1)
    own_domain = lax.dynamic_slice_in_dim(domain_rows, column_offset, pair_columns, 1).reshape(
        own_pairs, domain_size
    )
    own_basis = pno_basis.reshape(own_pairs, domain_size, width)
    local_rows = jnp.arange(pair_rows, dtype=jnp.int32)[:, None, None]
    local_columns = jnp.arange(pair_columns, dtype=jnp.int32)[None, :, None]
    row_slots = (row_neighbours * pair_columns + local_columns).reshape(own_pairs, -1)
    column_slots = (local_rows * total_columns + column_neighbours).reshape(own_pairs, -1)
    row_live = (
        jnp.arange(row_neighbours.shape[2], dtype=jnp.int32)[None, None, :] < row_counts[:, :, None]
    )
    row_table = jnp.broadcast_to(coupling_rows[:, None, :], (pair_rows, pair_columns, total_rows))
    row_weight = jnp.where(row_live, jnp.take_along_axis(row_table, row_neighbours, axis=2), 0.0)
    column_live = (
        jnp.arange(column_neighbours.shape[2], dtype=jnp.int32)[None, None, :]
        < column_counts[:, :, None]
    )
    column_table = coupling_columns.T[None, :, :]
    column_weight = jnp.where(
        column_live, jnp.take_along_axis(column_table, column_neighbours, axis=2), 0.0
    )
    weights = jnp.concatenate(
        [row_weight.reshape(own_pairs, -1), column_weight.reshape(own_pairs, -1)], axis=1
    )
    partner_domains = jnp.concatenate(
        [
            domain_columns.reshape(total_rows * pair_columns, domain_size)[row_slots],
            domain_rows.reshape(pair_rows * total_columns, domain_size)[column_slots],
        ],
        axis=1,
    )

    def slot_pick(column_slab, row_slab):
        column_flat = column_slab.reshape(
            (column_slab.shape[0] * column_slab.shape[1],) + column_slab.shape[2:]
        )
        row_flat = row_slab.reshape((row_slab.shape[0] * row_slab.shape[1],) + row_slab.shape[2:])
        return jnp.concatenate([column_flat[row_slots], row_flat[column_slots]], axis=1)

    energy_gap = (
        pno_energy[:, :, :, None]
        + pno_energy[:, :, None, :]
        - row_energy[:, None, None, None]
        - column_energy[None, :, None, None]
    )
    column_bases = gathered_copies(pno_basis, "ia", 0)
    row_bases = lax.all_gather(pno_basis, "ja", axis=1, tiled=True)
    partner_bases = slot_pick(column_bases, row_bases)
    stored = lax.map(pair_intersections, (own_domain, own_basis, partner_domains, partner_bases))
    current = amplitudes
    for iteration in range(ITERS):
        rounded = current.astype(jnp.bfloat16)
        column_rounded = gathered_copies(rounded, "ia", 0)
        row_rounded = lax.all_gather(rounded, "ja", axis=1, tiled=True)
        intersection_wide = stored.astype(jnp.float32)
        halved = jnp.einsum(
            "psab,psbc->psac",
            intersection_wide,
            slot_pick(column_rounded, row_rounded).astype(jnp.float32),
        ).astype(jnp.bfloat16)
        projected = jnp.einsum("psac,psdc->psad", halved.astype(jnp.float32), intersection_wide)
        coupled = jnp.sum(weights[:, :, None, None] * projected, axis=1).reshape(
            pair_rows, pair_columns, width, width
        )
        residual = exchange_ints + energy_gap * current - coupled
        current = current - residual / (energy_gap + level_shift)
    pair_energy = jnp.sum(
        exchange_ints * (2.0 * current - jnp.swapaxes(current, 2, 3)), axis=(2, 3)
    )
    return (current, pair_energy)


def solution(mesh):
    in_specs = (
        P("ia", "ja", None, None),
        P(),
        P("ia", "ja", None, None),
        P("ia", "ja", None, None),
        P("ia", "ja", None),
        P("ia"),
        P("ja"),
        P("ia", None),
        P(None, "ja"),
        P("ia", "ja", None),
        P("ia", "ja", None),
        P("ia", "ja"),
        P("ia", "ja"),
    )
    out_specs = (P("ia", "ja", None, None), P("ia", "ja"))
    return jax.shard_map(local, mesh=mesh, in_specs=in_specs, out_specs=out_specs, check_vma=False)
```

profile of v0, /device:TPU:1, one launch (start us, length us, event | category | flops | bytes accessed | tf_op | source)
XLA Modules:
  0.0 222.9 jit_solution(1346246131528462927)
XLA Ops:
  7.2 1.6 bitcast_convert_fusion
  8.9 0.7 all-gather.4.cloned.1.call-update
  9.6 0.9 fusion.78
  10.7 25.0 %all_to_all.15 = bf16[8,1,2,128,128]{4,3,2,1,0:T(8,128)(2,1)} all-to-all(bf16[8,1,2,128,128]{4,3,2,1,0:T(8,128)(2,1)S(1)} %broadcast_in_dim.72), channel_id=1, replica_groups=mesh['ia'=8,'ja'=32] {'ia'}, dimensions={0} | all-to-all | bytes 1048576 | tf_op jit(solution)/shard_map/all_to_all | solution.py:12
  35.7 1.7 broadcast_in_dim.43
  37.4 3.7 %all-to-all-start = ((bf16[8,1,2,512,128]{4,3,2,1,0:T(8,128)(2,1)}), bf16[8,1,2,512,128]{4,3,2,1,0:T(8,128)(2,1)S(1)}, u32[]{:S(2)}, u32[]{:S(2)}) async-start(bf16[8,1,2,512,128]{4,3,2,1,0:T(8,128)(2,1)} %broadcast_in_dim.43), calls=%async_computation | async-start | bytes 4194304 | tf_op jit(solution)/shard_map/all_to_all | solution.py:12
  42.8 0.7 gather_fusion.8
  44.2 1.1 gather_fusion.9
  46.6 1.3 gather_fusion.1
  47.9 0.7 fusion.66
  48.6 0.7 fusion.67
  49.4 0.9 pad_add_fusion
  50.3 2.4 %gather_fusion.4 = bf16[12,128,128]{2,1,0:T(8,128)(2,1)} fusion(bf16[16,128,128]{2,1,0:T(8,128)(2,1)} %bitcast.136, s32[1024]{0:T(1024)S(1)} %pad_clamp_fusion.1), kind=kCustom, calls=%fused_computation.4 | custom fusion | bytes 786480 | tf_op jit(solution)/shard_map/gather | solution.py:100
  52.7 40.0 %all-to-all-done = bf16[8,1,2,512,128]{4,3,2,1,0:T(8,128)(2,1)S(1)} async-done(((bf16[8,1,2,512,128]{4,3,2,1,0:T(8,128)(2,1)}), bf16[8,1,2,512,128]{4,3,2,1,0:T(8,128)(2,1)S(1)}, u32[]{:S(2)}, u32[]{:S(2)}) %all-to-all-start) | async-done | bytes 2097184 | tf_op jit(solution)/shard_map/all_to_all | solution.py:12
  92.8 1.9 gather_fusion.2
  94.7 3.6 %gather_fusion.5 = bf16[48,128,128]{2,1,0:T(8,128)(2,1)} fusion(bf16[64,128,128]{2,1,0:T(8,128)(2,1)} %bitcast.140, s32[1024]{0:T(1024)S(1)} %pad_clamp_fusion), kind=kCustom, calls=%fused_computation.5 | custom fusion | bytes 3145920 | tf_op jit(solution)/shard_map/gather | solution.py:100
  98.3 24.7 %all-gather.4.cloned.1.call-done = bf16[1,64,512,128]{3,2,0,1:T(8,128)(2,1)} async-done(((bf16[1,2,512,128]{3,2,0,1:T(8,128)(2,1)}), bf16[1,64,512,128]{3,2,0,1:T(8,128)(2,1)}) %all-gather.4.cloned.1.call-update) | async-done | bytes 8388624 | tf_op jit(solution)/shard_map/all_gather | solution.py:109
  122.9 8.5 %gather_fusion.3 = bf16[48,512,128]{2,1,0:T(8,128)(2,1)} fusion(bf16[64,512,128]{2,1,0:T(8,128)(2,1)} %bitcast.135, s32[1024]{0:T(1024)S(1)} %pad_clamp_fusion), kind=kCustom, calls=%fused_computation.3 | custom fusion | bytes 12583104 | tf_op jit(solution)/shard_map/gather | solution.py:100
  131.5 6.5 %pad_maximum_fusion = bf16[2,30,512,128]{3,2,1,0:T(8,128)(2,1)} fusion(bf16[2,24,512,128]{3,2,1,0:T(8,128)(2,1)} %bitcast.132, bf16[2,6,512,128]{3,2,1,0:T(8,128)(2,1)S(1)} %bitcast.134), kind=kLoop, calls=%fused_computation.26 | loop fusion | flops 3932160 | bytes 15728640 | tf_op jit(solution)/shard_map/concatenate | solution.py:100
  138.0 17.2 %while.10 = (s32[]{:T(128)}, bf16[2,30,128,128]{2,3,1,0:T(8,128)(2,1)}, s32[2,512]{1,0:T(2,128)S(1)}, s32[2,30,512]{2,1,0:T(8,128)S(1)}, bf16[2,30,512,128]{3,2,...) while((s32[]{:T(128)}, bf16[2,30,128,128]{2,3,1,0:T(8,128)(2,1)}, s32[2,512]{1,0:T(2,128)S(1)}, ...), condition=%wide.region_1.2_spmd, body=%wide.region_0.0_spmd.sunk | while | flops 2526904320 | bytes 5242453 | solution.py:111
  138.0 8.6 %fusion.88 = bf16[2,30,128,128]{2,3,1,0:T(8,128)(2,1)} fusion(bf16[2,30,128,128]{2,3,1,0:T(8,128)(2,1)} %get-tuple-element.100, s32[]{:T(128)} %get-tuple-element.99, bf16[2,30,512,128]{3,2,1,0:T(8,128)(2,1)} %get-tuple-element.110, s32[30,512]{1,0:T(8,128)S(1)} %dynamic-slice_bitcast_fusion.4, s32[512]{0:T(512)S(1)} %bitcast.150, ...), kind=kOutput, calls=%fused_computation.20.clone.1 | convolution fusion | flops 2526904320 | bytes 5115392 | tf_op jit(solution)/shard_map/while/body/eval_jaxpr/ua,sub->sab/dot_general | solution.py:32
  146.6 8.5 %fusion.88 = bf16[2,30,128,128]{2,3,1,0:T(8,128)(2,1)} fusion(bf16[2,30,128,128]{2,3,1,0:T(8,128)(2,1)} %get-tuple-element.100, s32[]{:T(128)} %get-tuple-element.99, bf16[2,30,512,128]{3,2,1,0:T(8,128)(2,1)} %get-tuple-element.110, s32[30,512]{1,0:T(8,128)S(1)} %dynamic-slice_bitcast_fusion.4, s32[512]{0:T(512)S(1)} %bitcast.150, ...), kind=kOutput, calls=%fused_computation.20.clone.1 | convolution fusion | flops 2526904320 | bytes 5115392 | tf_op jit(solution)/shard_map/while/body/eval_jaxpr/ua,sub->sab/dot_general | solution.py:32
  155.2 3.6 %multiply_reduce_fusion.1 = f32[2,128,128]{2,1,0:T(8,128)S(1)} fusion(bf16[2,30,128,128]{2,3,1,0:T(8,128)(2,1)} %get-tuple-element.34, f32[2,30]{1,0:T(2,128)S(1)} %pad_maximum_fusion.1, bf16[2,24,128,128]{3,2,1,0:T(8,128)(2,1)S(1)} %bitcast.138, bf16[2,6,128,128]{3,2,1,0:T(8,128)(2,1)} %bitcast.147), kind=kOutput, calls=%fused_computation.28 | convolution fusion | flops 507215872 | bytes 4063472 | tf_op jit(solution)/shard_map/psac,psdc->psad/dot_general | solution.py:123
  158.9 0.8 fusion.72
  159.7 1.7 broadcast_in_dim.73
  161.4 6.7 %all-to-all-start.2 = ((bf16[8,1,2,128,128]{4,3,2,1,0:T(8,128)(2,1)}), bf16[8,1,2,128,128]{4,3,2,1,0:T(8,128)(2,1)S(1)}, u32[]{:S(2)}, u32[]{:S(2)}) async-start(bf16[8,1,2,128,128]{4,3,2,1,0:T(8,128)(2,1)} %broadcast_in_dim.73), calls=%async_computation.2 | async-start | bytes 1048576 | tf_op jit(solution)/shard_map/all_to_all | solution.py:12
  168.2 17.9 %all-to-all-done.2 = bf16[8,1,2,128,128]{4,3,2,1,0:T(8,128)(2,1)S(1)} async-done(((bf16[8,1,2,128,128]{4,3,2,1,0:T(8,128)(2,1)}), bf16[8,1,2,128,128]{4,3,2,1,0:T(8,128)(2,1)S(1)}, u32[]{:S(2)}, u32[]{:S(2)}) %all-to-all-start.2) | async-done | bytes 524320 | tf_op jit(solution)/shard_map/all_to_all | solution.py:12
  186.7 21.3 %all-gather.8.cloned.1.call-done = bf16[1,64,128,128]{3,2,0,1:T(8,128)(2,1)} async-done(((bf16[1,2,128,128]{3,2,0,1:T(8,128)(2,1)}), bf16[1,64,128,128]{3,2,0,1:T(8,128)(2,1)}) %all-gather.8.cloned.1.call-update) | async-done | bytes 2097168 | tf_op jit(solution)/shard_map/all_gather | solution.py:116
  208.0 2.4 %gather_fusion.7 = bf16[48,128,128]{2,1,0:T(8,128)(2,1)S(1)} fusion(bf16[64,128,128]{2,1,0:T(8,128)(2,1)} %bitcast.141, s32[1024]{0:T(1024)S(1)} %pad_clamp_fusion), kind=kCustom, calls=%fused_computation.7 | custom fusion | bytes 3145920 | tf_op jit(solution)/shard_map/gather | solution.py:100
  210.5 4.1 %multiply_reduce_fusion = f32[2,128,128]{2,1,0:T(8,128)} fusion(bf16[2,30,128,128]{2,3,1,0:T(8,128)(2,1)} %get-tuple-element.34, f32[2,30]{1,0:T(2,128)S(1)} %pad_maximum_fusion.1, bf16[2,24,128,128]{3,2,1,0:T(8,128)(2,1)S(1)} %bitcast.139, bf16[2,6,128,128]{3,2,1,0:T(8,128)(2,1)S(1)} %bitcast.148), kind=kOutput, calls=%fused_computation.27 | convolution fusion | flops 507215872 | bytes 4063472 | tf_op jit(solution)/shard_map/psac,psdc->psad/dot_general | solution.py:123
  214.6 1.0 fusion.62
  215.8 0.6 fusion.60
  (59 shorter events, 4.1 us)
Async XLA Ops:
  7.2 34.2 %copy-start = (s32[8,64,512]{2,1,0:T(8,128)S(1)}, s32[8,64,512]{2,1,0:T(8,128)}, u32[]{:S(2)}) copy-start(s32[8,64,512]{2,1,0:T(8,128)} %param.16) | copy-start | bytes 3145732
  7.2 28.5 %copy-start.7 = (bf16[1,2,512,128]{3,2,1,0:T(8,128)(2,1)S(1)}, bf16[1,2,512,128]{3,2,1,0:T(8,128)(2,1)}, u32[]{:S(2)}) copy-start(bf16[1,2,512,128]{3,2,1,0:T(8,128)(2,1)} %param.15) | copy-start | bytes 786436
  7.2 87.5 %all-gather.6.cloned.1.call-start = ((), (), s32[]{:S(2)}) async-start(), calls=%async_computation.4 | async-start | bytes 2162688 | tf_op jit(solution)/shard_map/all_gather | solution.py:116
  8.9 114.0 %all-gather.4.cloned.1.call-start = ((), (), s32[]{:S(2)}) async-start(), calls=%async_computation.3 | async-start | bytes 8650752 | tf_op jit(solution)/shard_map/all_gather | solution.py:109
  37.4 3.8 %copy-start.10 = (s32[1,2,24]{2,1,0:T(2,128)S(1)}, s32[1,2,24]{2,1,0:T(2,128)}, u32[]{:S(2)}) copy-start(s32[1,2,24]{2,1,0:T(2,128)} %param.25) | copy-start | bytes 580
  37.4 4.0 %copy-start.9 = (s32[1,2,6]{2,1,0:T(2,128)S(1)}, s32[1,2,6]{2,1,0:T(2,128)}, u32[]{:S(2)}) copy-start(s32[1,2,6]{2,1,0:T(2,128)} %param.24) | copy-start | bytes 148
  37.4 5.4 %copy-start.12 = (f32[1,8]{1,0:T(1,128)S(1)}, f32[1,8]{1,0:T(1,128)}, u32[]{:S(2)}) copy-start(f32[1,8]{1,0:T(1,128)} %param.22) | copy-start | bytes 100
  37.4 6.8 %copy-start.1 = (f32[64,2]{0,1:T(2,128)S(1)}, f32[64,2]{0,1:T(2,128)}, u32[]{:S(2)}) copy-start(f32[64,2]{0,1:T(2,128)} %param.23) | copy-start | bytes 1540
  37.4 55.3 %all-to-all-start = ((bf16[8,1,2,512,128]{4,3,2,1,0:T(8,128)(2,1)}), bf16[8,1,2,512,128]{4,3,2,1,0:T(8,128)(2,1)S(1)}, u32[]{:S(2)}, u32[]{:S(2)}) async-start(bf16[8,1,2,512,128]{4,3,2,1,0:T(8,128)(2,1)} %broadcast_in_dim.43), calls=%async_computation | async-start | bytes 4194304 | tf_op jit(solution)/shard_map/all_to_all | solution.py:12
  41.2 166.8 %all-gather.8.cloned.1.call-start = ((), (), s32[]{:S(2)}) async-start(), calls=%async_computation.5 | async-start | bytes 2162688 | tf_op jit(solution)/shard_map/all_gather | solution.py:116
  122.9 8.5 %copy-start.2 = (bf16[12,512,128]{2,1,0:T(8,128)(2,1)S(1)}, bf16[12,512,128]{2,1,0:T(8,128)(2,1)}, u32[]{:S(2)}) copy-start(bf16[12,512,128]{2,1,0:T(8,128)(2,1)} %gather_fusion.2) | copy-start | bytes 4718596
  138.0 17.2 %copy-start.3 = (bf16[48,128,128]{2,1,0:T(8,128)(2,1)S(1)}, bf16[48,128,128]{2,1,0:T(8,128)(2,1)}, u32[]{:S(2)}) copy-start(bf16[48,128,128]{2,1,0:T(8,128)(2,1)} %gather_fusion.5) | copy-start | bytes 4718596
  155.1 3.7 %copy-start.4 = (f32[1,2,128,128]{3,2,1,0:T(8,128)S(1)}, f32[1,2,128,128]{3,2,1,0:T(8,128)}, u32[]{:S(2)}) copy-start(f32[1,2,128,128]{3,2,1,0:T(8,128)} %param.17) | copy-start | bytes 393220
  155.1 3.7 %copy-start.6 = (f32[1,2,128,128]{3,2,1,0:T(8,128)S(1)}, f32[1,2,128,128]{3,2,1,0:T(8,128)}, u32[]{:S(2)}) copy-start(f32[1,2,128,128]{3,2,1,0:T(8,128)} %param.18) | copy-start | bytes 393220
  155.1 3.7 %copy-start.8 = (f32[1,2,128]{2,1,0:T(2,128)S(1)}, f32[1,2,128]{2,1,0:T(2,128)}, u32[]{:S(2)}) copy-start(f32[1,2,128]{2,1,0:T(2,128)} %param.19) | copy-start | bytes 3076
  155.1 3.7 %copy-start.11 = (f32[2]{0:T(128)S(1)}, f32[2]{0:T(128)}, u32[]{:S(2)}) copy-start(f32[2]{0:T(128)} %param.21) | copy-start | bytes 28
  161.4 24.7 %all-to-all-start.2 = ((bf16[8,1,2,128,128]{4,3,2,1,0:T(8,128)(2,1)}), bf16[8,1,2,128,128]{4,3,2,1,0:T(8,128)(2,1)S(1)}, u32[]{:S(2)}, u32[]{:S(2)}) async-start(bf16[8,1,2,128,128]{4,3,2,1,0:T(8,128)(2,1)} %broadcast_in_dim.73), calls=%async_computation.2 | async-start | bytes 1048576 | tf_op jit(solution)/shard_map/all_to_all | solution.py:12
  215.7 0.7 copy-start.5
Sparse Core Ops, SparseCore 0:
  10.6 52.7 all-gather.5
  65.9 56.9 all-gather.3
  159.8 48.2 all-gather.7
where the time goes:
time: 224 us; the launch traced here: 223 us
  waiting for transfers between devices  105 us (47%)
  local copies, waits for them, and re-layouts  29.2 us (13%)
  blocking collectives  25 us (11%)
  matrix products  24.9 us (11%)
  between operations  14.6 us (7%)
  other arithmetic  14 us (6%)
  starting transfers between devices  10.6 us (5%)
    all_to_all x2, waiting for transfers between devices, sent_to_all(): return lax.all_to_all(copies, axis, split_axis=0, concat_axis=0, tiled=True)  57.9 us
    all_to_all x1, blocking collectives, sent_to_all(): return lax.all_to_all(copies, axis, split_axis=0, concat_axis=0, tiled=True)  25 us
    all_gather x1, waiting for transfers between devices, local(): row_bases = lax.all_gather(pno_basis, 'ja', axis=1, tiled=True)  24.7 us
    all_gather x2, waiting for transfers between devices, local(): row_rounded = lax.all_gather(rounded, 'ja', axis=1, tiled=True)  21.3 us
    dot_general x2, matrix products, pair_intersections(): jnp.einsum('ua,sub->sab', own_basis, picked, preferred_element_type=jnp.f...  17.1 us
    gather x3, local copies, waits for them, and re-layouts, slot_pick(): row_flat[column_slots]  14.5 us
    all_to_all x2, starting transfers between devices, sent_to_all(): return lax.all_to_all(copies, axis, split_axis=0, concat_axis=0, tiled=True)  10.5 us
    dot_general x2, matrix products, local(): jnp.einsum('psac,psdc->psad', halved.astype(jnp.float32), intersection_wide)  7.79 us
  transfers between devices with their start and end apart: 5, of which 4 were waited for; matrix products, arithmetic and copies ran while one was open for 10% of the time, Pallas kernels for 0%

commit v1 on v0

--- a/solution.py
+++ b/solution.py
@@ -113,7 +113,9 @@
     for iteration in range(ITERS):
         rounded = current.astype(jnp.bfloat16)
         column_rounded = gathered_copies(rounded, "ia", 0)
-        row_rounded = lax.all_gather(rounded, "ja", axis=1, tiled=True)
+        row_rounded = jnp.concatenate(
+            lax.all_to_all(jnp.stack([rounded] * lax.axis_size("ja")), "ja", 0, 0), axis=1
+        )
         intersection_wide = stored.astype(jnp.float32)
         halved = jnp.einsum(
             "psab,psbc->psac",

time: 224 us -> 253 us (1.13)
  blocking collectives: 25 us -> 96.8 us
  waiting for transfers between devices: 105 us -> 59.3 us
  starting transfers between devices: 10.6 us -> 13.9 us
  other arithmetic: 14 us -> 11.4 us
    all_to_all x0 -> x1, blocking collectives: none -> 52.4 us  [local(): lax.all_to_all(jnp.stack([rounded] * lax.axis_size('ja')), 'ja', 0, 0)]
    all_to_all x0 -> x1, waiting for transfers between devices: none -> 26.1 us  [local(): lax.all_to_all(jnp.stack([rounded] * lax.axis_size('ja')), 'ja', 0, 0)]
    all_to_all x2 -> x1, waiting for transfers between devices: 57.9 us -> 32.5 us  [sent_to_all(): return lax.all_to_all(copies, axis, split_axis=0, concat_axis=0, tiled=True)]
    all_gather x1, waiting for transfers between devices: 24.7 us -> 0.01 us  [local(): row_bases = lax.all_gather(pno_basis, 'ja', axis=1, tiled=True)]
    all_gather x2 -> x0, waiting for transfers between devices: 21.3 us -> none  [local(): row_rounded = lax.all_gather(rounded, 'ja', axis=1, tiled=True)]
    all_to_all x1 -> x2, blocking collectives: 25 us -> 44.4 us  [sent_to_all(): return lax.all_to_all(copies, axis, split_axis=0, concat_axis=0, tiled=True)]
    all_to_all x0 -> x1, starting transfers between devices: none -> 10.1 us  [local(): lax.all_to_all(jnp.stack([rounded] * lax.axis_size('ja')), 'ja', 0, 0)]
    all_to_all x2 -> x1, starting transfers between devices: 10.5 us -> 3.75 us  [sent_to_all(): return lax.all_to_all(copies, axis, split_axis=0, concat_axis=0, tiled=True)]
  transfers between devices with their start and end apart: 5 -> 3, of which waited for: 4 -> 2; matrix products, arithmetic and copies ran while one was open for 10% -> 9% of each run, Pallas kernels for 0% -> 0%
where the time goes in v1:
time: 253 us; the launch traced here: 252 us
  blocking collectives  96.8 us (38%)
  waiting for transfers between devices  59.3 us (23%)
  local copies, waits for them, and re-layouts  31.3 us (12%)
  matrix products  24.9 us (10%)
  between operations  15 us (6%)
  starting transfers between devices  13.9 us (5%)
  other arithmetic  11.4 us (5%)
    all_to_all x1, blocking collectives, local(): lax.all_to_all(jnp.stack([rounded] * lax.axis_size('ja')), 'ja', 0, 0)  52.4 us
    all_to_all x2, blocking collectives, sent_to_all(): return lax.all_to_all(copies, axis, split_axis=0, concat_axis=0, tiled=True)  44.4 us
    all_to_all x1, waiting for transfers between devices, sent_to_all(): return lax.all_to_all(copies, axis, split_axis=0, concat_axis=0, tiled=True)  32.5 us
    all_to_all x1, waiting for transfers between devices, local(): lax.all_to_all(jnp.stack([rounded] * lax.axis_size('ja')), 'ja', 0, 0)  26.1 us
    dot_general x2, matrix products, pair_intersections(): jnp.einsum('ua,sub->sab', own_basis, picked, preferred_element_type=jnp.f...  17.1 us
    gather x3, local copies, waits for them, and re-layouts, slot_pick(): row_flat[column_slots]  14 us
    all_to_all x1, starting transfers between devices, local(): lax.all_to_all(jnp.stack([rounded] * lax.axis_size('ja')), 'ja', 0, 0)  10.1 us
    dot_general x2, matrix products, local(): jnp.einsum('psac,psdc->psad', halved.astype(jnp.float32), intersection_wide)  7.75 us
  transfers between devices with their start and end apart: 3, of which 2 were waited for; matrix products, arithmetic and copies ran while one was open for 9% of the time, Pallas kernels for 0%

profile of v1, /device:TPU:1, one launch (start us, length us, event | category | flops | bytes accessed | tf_op | source)
XLA Modules:
  0.0 252.5 jit_solution(17118645493353227879)
XLA Ops:
  7.2 0.7 all-gather.2.cloned.1.call-update
  7.9 0.9 convert_bitcast_fusion.1
  8.9 25.0 %all_to_all.25 = bf16[8,1,2,128,128]{4,3,2,1,0:T(8,128)(2,1)} all-to-all(bf16[8,1,2,128,128]{4,3,2,1,0:T(8,128)(2,1)S(1)} %broadcast_in_dim.72), channel_id=1, replica_groups=mesh['ia'=8,'ja'=32] {'ia'}, dimensions={0} | all-to-all | bytes 1048576 | tf_op jit(solution)/shard_map/all_to_all | solution.py:12
  34.5 52.4 %all_to_all.26 = bf16[32,1,2,128,128]{4,3,2,1,0:T(8,128)(2,1)} all-to-all(bf16[32,1,2,128,128]{4,3,2,1,0:T(8,128)(2,1)S(1)} %stack.4), channel_id=1, replica_groups=mesh['ia'=8,'ja'=32] {'ja'}, dimensions={0} | all-to-all | bytes 4194304 | tf_op jit(solution)/shard_map/all_to_all | solution.py:117
  86.9 1.8 broadcast_in_dim.43
  88.7 3.7 %all-to-all-start = ((bf16[8,1,2,512,128]{4,3,2,1,0:T(8,128)(2,1)}), bf16[8,1,2,512,128]{4,3,2,1,0:T(8,128)(2,1)S(1)}, u32[]{:S(2)}, u32[]{:S(2)}) async-start(bf16[8,1,2,512,128]{4,3,2,1,0:T(8,128)(2,1)} %broadcast_in_dim.43), calls=%async_computation | async-start | bytes 4194304 | tf_op jit(solution)/shard_map/all_to_all | solution.py:12
  94.0 0.7 gather_fusion.8
  94.7 0.7 reshape.334
  95.5 1.1 gather_fusion.9
  96.6 0.7 reshape.342
  97.9 1.3 gather_fusion.1
  99.2 0.7 fusion.66
  99.9 0.7 fusion.67
  101.3 0.9 pad_add_fusion
  102.2 2.4 gather_fusion.4
  104.6 3.5 %gather_fusion.5 = bf16[48,128,128]{2,1,0:T(8,128)(2,1)} fusion(bf16[64,128,128]{2,1,0:T(8,128)(2,1)} %bitcast.114, s32[1024]{0:T(1024)S(1)} %pad_clamp_fusion), kind=kCustom, calls=%fused_computation.5 | custom fusion | bytes 3145920 | tf_op jit(solution)/shard_map/gather | solution.py:100
  108.1 32.5 %all-to-all-done = bf16[8,1,2,512,128]{4,3,2,1,0:T(8,128)(2,1)S(1)} async-done(((bf16[8,1,2,512,128]{4,3,2,1,0:T(8,128)(2,1)}), bf16[8,1,2,512,128]{4,3,2,1,0:T(8,128)(2,1)S(1)}, u32[]{:S(2)}, u32[]{:S(2)}) %all-to-all-start) | async-done | bytes 2097184 | tf_op jit(solution)/shard_map/all_to_all | solution.py:12
  140.6 1.9 gather_fusion.2
  142.6 8.5 %gather_fusion.3 = bf16[48,512,128]{2,1,0:T(8,128)(2,1)} fusion(bf16[64,512,128]{2,1,0:T(8,128)(2,1)} %bitcast.117, s32[1024]{0:T(1024)S(1)} %pad_clamp_fusion), kind=kCustom, calls=%fused_computation.3 | custom fusion | bytes 12583104 | tf_op jit(solution)/shard_map/gather | solution.py:100
  151.1 6.5 %pad_maximum_fusion = bf16[2,30,512,128]{3,2,1,0:T(8,128)(2,1)} fusion(bf16[2,24,512,128]{3,2,1,0:T(8,128)(2,1)} %bitcast.112, bf16[2,6,512,128]{3,2,1,0:T(8,128)(2,1)S(1)} %bitcast.116), kind=kLoop, calls=%fused_computation.26 | loop fusion | flops 3932160 | bytes 15728640 | tf_op jit(solution)/shard_map/concatenate | solution.py:100
  157.6 17.2 %while.10 = (s32[]{:T(128)}, bf16[2,30,128,128]{2,3,1,0:T(8,128)(2,1)}, s32[2,512]{1,0:T(2,128)S(1)}, s32[2,30,512]{2,1,0:T(8,128)S(1)}, bf16[2,30,512,128]{3,2,...) while((s32[]{:T(128)}, bf16[2,30,128,128]{2,3,1,0:T(8,128)(2,1)}, s32[2,512]{1,0:T(2,128)S(1)}, ...), condition=%wide.region_1.2_spmd, body=%wide.region_0.0_spmd.sunk | while | flops 2526904320 | bytes 5242453 | solution.py:111
  157.6 8.6 %fusion.86 = bf16[2,30,128,128]{2,3,1,0:T(8,128)(2,1)} fusion(bf16[2,30,128,128]{2,3,1,0:T(8,128)(2,1)} %get-tuple-element.98, s32[]{:T(128)} %get-tuple-element.97, bf16[2,30,512,128]{3,2,1,0:T(8,128)(2,1)} %get-tuple-element.108, s32[30,512]{1,0:T(8,128)S(1)} %dynamic-slice_bitcast_fusion.4, s32[512]{0:T(512)S(1)} %bitcast.128, ...), kind=kOutput, calls=%fused_computation.20.clone.1 | convolution fusion | flops 2526904320 | bytes 5115392 | tf_op jit(solution)/shard_map/while/body/eval_jaxpr/ua,sub->sab/dot_general | solution.py:32
  166.3 8.5 %fusion.86 = bf16[2,30,128,128]{2,3,1,0:T(8,128)(2,1)} fusion(bf16[2,30,128,128]{2,3,1,0:T(8,128)(2,1)} %get-tuple-element.98, s32[]{:T(128)} %get-tuple-element.97, bf16[2,30,512,128]{3,2,1,0:T(8,128)(2,1)} %get-tuple-element.108, s32[30,512]{1,0:T(8,128)S(1)} %dynamic-slice_bitcast_fusion.4, s32[512]{0:T(512)S(1)} %bitcast.128, ...), kind=kOutput, calls=%fused_computation.20.clone.1 | convolution fusion | flops 2526904320 | bytes 5115392 | tf_op jit(solution)/shard_map/while/body/eval_jaxpr/ua,sub->sab/dot_general | solution.py:32
  174.8 3.7 %multiply_reduce_fusion.1 = f32[2,128,128]{2,1,0:T(8,128)S(1)} fusion(bf16[2,30,128,128]{2,3,1,0:T(8,128)(2,1)} %get-tuple-element.34, f32[2,30]{1,0:T(2,128)S(1)} %copy-done.12, bf16[2,24,128,128]{3,2,1,0:T(8,128)(2,1)S(1)} %bitcast.120, bf16[2,6,128,128]{3,2,1,0:T(8,128)(2,1)} %bitcast.125), kind=kOutput, calls=%fused_computation.28 | convolution fusion | flops 507215872 | bytes 4063472 | tf_op jit(solution)/shard_map/psac,psdc->psad/dot_general | solution.py:125
  178.8 19.4 %all_to_all.27 = bf16[8,1,2,128,128]{4,3,2,1,0:T(8,128)(2,1)} all-to-all(bf16[8,1,2,128,128]{4,3,2,1,0:T(8,128)(2,1)S(1)} %broadcast_in_dim.73), channel_id=1, replica_groups=mesh['ia'=8,'ja'=32] {'ia'}, dimensions={0} | all-to-all | bytes 1048576 | tf_op jit(solution)/shard_map/all_to_all | solution.py:12
  198.1 1.9 stack.5
  200.0 10.1 %all-to-all-start.4 = ((bf16[32,1,2,128,128]{4,3,2,1,0:T(8,128)(2,1)}), bf16[32,1,2,128,128]{4,3,2,1,0:T(8,128)(2,1)S(1)}, u32[]{:S(2)}, u32[]{:S(2)}) async-start(bf16[32,1,2,128,128]{4,3,2,1,0:T(8,128)(2,1)} %stack.5), calls=%async_computation.4 | async-start | bytes 4194304 | tf_op jit(solution)/shard_map/all_to_all | solution.py:117
  210.2 2.4 gather_fusion.6
  212.6 26.1 %all-to-all-done.4 = bf16[32,1,2,128,128]{4,3,2,1,0:T(8,128)(2,1)S(1)} async-done(((bf16[32,1,2,128,128]{4,3,2,1,0:T(8,128)(2,1)}), bf16[32,1,2,128,128]{4,3,2,1,0:T(8,128)(2,1)S(1)}, u32[]{:S(2)}, u32[]{:S(2)}) %all-to-all-start.4) | async-done | bytes 2097184 | tf_op jit(solution)/shard_map/all_to_all | solution.py:117
  238.7 2.0 gather_fusion.7
  240.7 4.1 %multiply_reduce_fusion = f32[2,128,128]{2,1,0:T(8,128)S(1)} fusion(bf16[2,30,128,128]{2,3,1,0:T(8,128)(2,1)} %get-tuple-element.34, f32[2,30]{1,0:T(2,128)S(1)} %copy-done.13, bf16[2,24,128,128]{3,2,1,0:T(8,128)(2,1)} %bitcast.121, bf16[2,6,128,128]{3,2,1,0:T(8,128)(2,1)} %bitcast.126), kind=kOutput, calls=%fused_computation.27 | convolution fusion | flops 507215872 | bytes 4063472 | tf_op jit(solution)/shard_map/psac,psdc->psad/dot_general | solution.py:125
  245.0 0.6 fusion.60
  (60 shorter events, 3.5 us)
Async XLA Ops:
  7.2 85.4 %copy-start = (s32[8,64,512]{2,1,0:T(8,128)S(1)}, s32[8,64,512]{2,1,0:T(8,128)}, u32[]{:S(2)}) copy-start(s32[8,64,512]{2,1,0:T(8,128)} %param.16) | copy-start | bytes 3145732
  7.2 135.4 %all-gather.2.cloned.1.call-start = ((), (), s32[]{:S(2)}) async-start(), calls=%async_computation.5 | async-start | bytes 8650752 | tf_op jit(solution)/shard_map/all_gather | solution.py:109
  34.5 52.4 %copy-start.6 = (bf16[1,2,512,128]{3,2,1,0:T(8,128)(2,1)S(1)}, bf16[1,2,512,128]{3,2,1,0:T(8,128)(2,1)}, u32[]{:S(2)}) copy-start(bf16[1,2,512,128]{3,2,1,0:T(8,128)(2,1)} %param.15) | copy-start | bytes 786436
  88.7 3.8 %copy-start.10 = (s32[1,2,24]{2,1,0:T(2,128)S(1)}, s32[1,2,24]{2,1,0:T(2,128)}, u32[]{:S(2)}) copy-start(s32[1,2,24]{2,1,0:T(2,128)} %param.25) | copy-start | bytes 580
  88.7 3.9 %copy-start.9 = (s32[1,2,6]{2,1,0:T(2,128)S(1)}, s32[1,2,6]{2,1,0:T(2,128)}, u32[]{:S(2)}) copy-start(s32[1,2,6]{2,1,0:T(2,128)} %param.24) | copy-start | bytes 148
  88.7 5.3 %copy-start.14 = (f32[1,8]{1,0:T(1,128)S(1)}, f32[1,8]{1,0:T(1,128)}, u32[]{:S(2)}) copy-start(f32[1,8]{1,0:T(1,128)} %param.22) | copy-start | bytes 100
  88.7 6.8 %copy-start.1 = (f32[64,2]{0,1:T(2,128)S(1)}, f32[64,2]{0,1:T(2,128)}, u32[]{:S(2)}) copy-start(f32[64,2]{0,1:T(2,128)} %param.23) | copy-start | bytes 1540
  88.7 51.9 %all-to-all-start = ((bf16[8,1,2,512,128]{4,3,2,1,0:T(8,128)(2,1)}), bf16[8,1,2,512,128]{4,3,2,1,0:T(8,128)(2,1)S(1)}, u32[]{:S(2)}, u32[]{:S(2)}) async-start(bf16[8,1,2,512,128]{4,3,2,1,0:T(8,128)(2,1)} %broadcast_in_dim.43), calls=%async_computation | async-start | bytes 4194304 | tf_op jit(solution)/shard_map/all_to_all | solution.py:12
  142.6 8.5 %copy-start.2 = (bf16[12,512,128]{2,1,0:T(8,128)(2,1)S(1)}, bf16[12,512,128]{2,1,0:T(8,128)(2,1)}, u32[]{:S(2)}) copy-start(bf16[12,512,128]{2,1,0:T(8,128)(2,1)} %gather_fusion.2) | copy-start | bytes 4718596
  157.6 17.2 %copy-start.3 = (bf16[48,128,128]{2,1,0:T(8,128)(2,1)S(1)}, bf16[48,128,128]{2,1,0:T(8,128)(2,1)}, u32[]{:S(2)}) copy-start(bf16[48,128,128]{2,1,0:T(8,128)(2,1)} %gather_fusion.5) | copy-start | bytes 4718596
  157.6 17.2 %copy-start.12 = (f32[2,30]{1,0:T(2,128)S(1)}, f32[2,30]{1,0:T(2,128)}, u32[]{:S(2)}) copy-start(f32[2,30]{1,0:T(2,128)} %pad_maximum_fusion.1) | copy-start | bytes 724
  174.8 3.7 %copy-start.5 = (f32[1,2,128,128]{3,2,1,0:T(8,128)S(1)}, f32[1,2,128,128]{3,2,1,0:T(8,128)}, u32[]{:S(2)}) copy-start(f32[1,2,128,128]{3,2,1,0:T(8,128)} %param.18) | copy-start | bytes 393220
  174.8 3.7 %copy-start.7 = (f32[1,2,128,128]{3,2,1,0:T(8,128)S(1)}, f32[1,2,128,128]{3,2,1,0:T(8,128)}, u32[]{:S(2)}) copy-start(f32[1,2,128,128]{3,2,1,0:T(8,128)} %param.17) | copy-start | bytes 393220
  174.8 3.7 %copy-start.8 = (f32[1,2,128]{2,1,0:T(2,128)S(1)}, f32[1,2,128]{2,1,0:T(2,128)}, u32[]{:S(2)}) copy-start(f32[1,2,128]{2,1,0:T(2,128)} %param.19) | copy-start | bytes 3076
  174.8 3.7 %copy-start.11 = (f32[2]{0:T(128)S(1)}, f32[2]{0:T(128)}, u32[]{:S(2)}) copy-start(f32[2]{0:T(128)} %param.21) | copy-start | bytes 28
  200.0 38.7 %all-to-all-start.4 = ((bf16[32,1,2,128,128]{4,3,2,1,0:T(8,128)(2,1)}), bf16[32,1,2,128,128]{4,3,2,1,0:T(8,128)(2,1)S(1)}, u32[]{:S(2)}, u32[]{:S(2)}) async-start(bf16[32,1,2,128,128]{4,3,2,1,0:T(8,128)(2,1)} %stack.5), calls=%async_computation.4 | async-start | bytes 4194304 | tf_op jit(solution)/shard_map/all_to_all | solution.py:117
  212.6 28.0 %copy-start.13 = (f32[2,30]{1,0:T(2,128)S(1)}, f32[2,30]{1,0:T(2,128)}, u32[]{:S(2)}) copy-start(f32[2,30]{1,0:T(2,128)} %pad_maximum_fusion.1) | copy-start | bytes 724
  244.9 0.7 copy-start.4
Sparse Core Ops, SparseCore 0:
  10.5 78.4 all-gather.1
